TPU v7x, 512 devices: a whole 4x8x8 slice. The times are simulated.
512 devices in a mesh: blk: 32 (over x_hi, z, core), adp: 16 (over y, x_lo).
Axes of the slice: x: 4 (x_hi: 2, x_lo: 2; x = x_hi * 2 + x_lo), y: 8, z: 8, core: 2. Of those that a mesh axis runs over, the one named last changes fastest.
Arguments:
- stream: bfloat16 [16384, 1536], P(('blk', 'adp')), may hold values from -6 to 6
- prenorm_gain: float32 [1536], replicated, may hold values from 0.25 to 1.75
- gate_up_weight: bfloat16 [2, 4608, 1536], P(None, 'blk'), may hold values from -0.15625 to 0.15625
- down_weight: bfloat16 [4608, 1536], P('blk'), may hold values from -0.09375 to 0.09375
- adapter_gate_input: bfloat16 [64, 32, 1536], P('adp'), may hold values from -0.15625 to 0.15625
- adapter_gate_output: bfloat16 [64, 2, 16, 4608], P('adp', None, None, 'blk'), may hold values from -0.75 to 0.75
- adapter_down_input: bfloat16 [64, 4608, 16], P('adp', 'blk'), may hold values from -0.09375 to 0.09375
- adapter_down_output: bfloat16 [64, 16, 1536], P('adp'), may hold values from -0.75 to 0.75
- adapter_of_request: int32 [256], replicated, may hold values from 0 to 63, as said below
- request_of_slot: int32 [16384], P(('blk', 'adp')), may hold values from 0 to 255
Outputs:
- mixed: bfloat16 [16384, 1536], P(('blk', 'adp'))
Inputs may be any that keep to these rules, and one draw needn't show every extreme that they name: `adapter_of_request`: exactly 16 distinct adapter numbers occur.
All inputs are finite; a program needn't handle non-finite values.
Results may differ from a plain program's by a relative error of at most 0.014.
Values may be sent and summed in bfloat16 or wider, within the bound.
A program may use at most 64 MiB of HBM per device.

v0:
```python
import jax
import jax.numpy as jnp
from jax import lax
from jax.sharding import PartitionSpec as P

ACTIVE = 16
norm_eps = 1e-06


def normalize(rows, gain):
    value_rows = rows.astype(jnp.float32)
    scale = lax.rsqrt(jnp.mean(value_rows * value_rows, axis=-1, keepdims=True) + norm_eps)
    return (value_rows * scale * gain).astype(jnp.bfloat16)


def local(
    stream,
    prenorm_gain,
    gate_up_weight,
    down_weight,
    adapter_gate_input,
    adapter_gate_output,
    adapter_down_input,
    adapter_down_output,
    adapter_of_request,
    request_of_slot,
):
    width = stream.shape[1]
    tok_rows = stream.shape[0]
    hidden_dev = down_weight.shape[0]
    rank_columns = adapter_down_output.shape[1]
    holders = lax.axis_size("adp")
    kept_rows = adapter_gate_input.shape[0]
    catalog = jnp.arange(kept_rows * holders, dtype=jnp.int32)
    used = jnp.any(adapter_of_request[:, None] == catalog[None, :], axis=0)
    order = jnp.cumsum(used.astype(jnp.int32)) - 1
    active_pos = jnp.arange(ACTIVE, dtype=jnp.int32)
    picked = used[None, :] & (order[None, :] == active_pos[:, None])
    active = jnp.sum(jnp.where(picked, catalog[None, :], 0), axis=1)
    every = (
        lax.all_gather(adapter_gate_input, "adp", axis=0, tiled=True),
        lax.all_gather(adapter_gate_output, "adp", axis=0, tiled=True),
        lax.all_gather(adapter_down_input, "adp", axis=0, tiled=True),
        lax.all_gather(adapter_down_output, "adp", axis=0, tiled=True),
    )
    input_factor = jnp.take(every[0], active, axis=0)
    output_factor = jnp.take(every[1], active, axis=0)
    down_input_factor = jnp.take(every[2], active, axis=0)
    down_output_factor = jnp.take(every[3], active, axis=0)
    table = jnp.arange(adapter_of_request.shape[0], dtype=jnp.int32)
    own_adapter = jnp.sum(
        jnp.where(request_of_slot[:, None] == table[None, :], adapter_of_request[None, :], 0),
        axis=1,
    )
    own_match = own_adapter[:, None] == active[None, :]
    own_slot = jnp.sum(jnp.where(own_match, active_pos[None, :], 0), axis=1)
    normed = normalize(stream, prenorm_gain)
    packed = jnp.concatenate(
        [normed, jnp.broadcast_to(own_slot.astype(jnp.bfloat16)[:, None], (tok_rows, 128))], axis=1
    )
    gathered = lax.all_gather(packed, "blk", axis=0, tiled=True)
    all_rows = gathered[:, :width]
    group_match = gathered[:, width : width + 1].astype(jnp.float32) == active_pos.astype(
        jnp.float32
    )
    match_ranks = jnp.repeat(group_match, rank_columns, axis=1)
    cat_rows = ACTIVE * rank_columns
    pre = []
    for side in range(2):
        rows_in = input_factor[:, side * rank_columns : (side + 1) * rank_columns]
        low = lax.dot_general(
            all_rows,
            rows_in.reshape(cat_rows, width),
            (((1,), (1,)), ((), ())),
            preferred_element_type=jnp.float32,
        )
        low_spread = jnp.where(match_ranks, low, 0).astype(jnp.bfloat16)
        base = lax.dot_general(
            all_rows,
            gate_up_weight[side],
            (((1,), (1,)), ((), ())),
            preferred_element_type=jnp.float32,
        )
        pre.append(
            base
            + jnp.dot(
                low_spread,
                output_factor[:, side].reshape(cat_rows, hidden_dev),
                preferred_element_type=jnp.float32,
            )
        )
    hidden = (jax.nn.gelu(pre[0], approximate=True) * pre[1]).astype(jnp.bfloat16)
    down_in = down_input_factor.transpose(1, 0, 2).reshape(hidden_dev, cat_rows)
    partial_value = jnp.dot(hidden, down_in, preferred_element_type=jnp.float32)
    low_spread = jnp.where(match_ranks, partial_value, 0).astype(jnp.bfloat16)
    part = jnp.dot(hidden, down_weight, preferred_element_type=jnp.float32) + jnp.dot(
        low_spread, down_output_factor.reshape(cat_rows, width), preferred_element_type=jnp.float32
    )
    total = lax.psum_scatter(
        part.astype(jnp.bfloat16), "blk", scatter_dimension=0, tiled=True
    ).astype(jnp.float32)
    return (stream.astype(jnp.float32) + total).astype(jnp.bfloat16)


def solution(mesh):
    in_specs = (
        P(("blk", "adp"), None),
        P(),
        P(None, "blk", None),
        P("blk", None),
        P("adp", None, None),
        P("adp", None, None, "blk"),
        P("adp", "blk", None),
        P("adp", None, None),
        P(),
        P(("blk", "adp")),
    )
    out_specs = P(("blk", "adp"), None)
    return jax.shard_map(local, mesh=mesh, in_specs=in_specs, out_specs=out_specs, check_vma=False)
```

profile of v0, /device:TPU:8, one launch (start us, length us, event | category | flops | bytes accessed | tf_op | source)
XLA Modules:
  0.0 529.4 jit_solution(233450659145894325)
XLA Ops:
  6.5 0.0 copy-start
  6.5 0.0 all-gather.8.cloned.1.call-start
  6.5 0.7 all-gather.8.cloned.1.call-update
  7.3 0.0 all-gather.4.cloned.1.call-start
  7.3 0.8 fusion.60
  8.1 0.1 copy.17
  8.2 0.1 reduce-window.8
  8.3 0.1 add_reduce_fusion
  8.4 0.1 select_reduce_fusion.2
  8.5 0.9 select_reduce_fusion
  9.4 0.1 select_reduce_fusion.1
  9.5 1.0 fusion.56
  10.5 1.0 fusion.58
  11.5 0.1 broadcast_in_dim.116
  11.6 0.7 pad_maximum_fusion
  12.3 0.0 all-gather.4.cloned.1.call-update
  12.3 0.0 all-gather.6.cloned.1.call-start
  12.3 0.7 all-gather.6.cloned.1.call-update
  13.0 0.0 reduce-scatter.2.cloned.1.call-start
  13.1 0.1 broadcast_in_dim.125
  13.2 0.1 broadcast_in_dim.126
  13.3 57.1 %all_gather.17 = bf16[64,2,16,144]{3,2,1,0:T(8,128)(2,1)S(1)} all-gather(bf16[4,2,16,144]{3,2,1,0:T(8,128)(2,1)} %param.15), channel_id=1, replica_groups=mesh['blk'=32,'adp'=16] {'adp'}, dimensions={0}, use_global_device_ids=true | all-gather | bytes 626688 | tf_op jit(solution)/shard_map/all_gather | solution.py:42
  70.3 0.6 gather_fusion.1
  70.9 46.0 %all_gather.18 = bf16[64,144,16]{1,2,0:T(8,128)(2,1)S(1)} all-gather(bf16[4,144,16]{1,2,0:T(8,128)(2,1)} %param.16), channel_id=1, replica_groups=mesh['blk'=32,'adp'=16] {'adp'}, dimensions={0}, use_global_device_ids=true | all-gather | bytes 313344 | tf_op jit(solution)/shard_map/all_gather | solution.py:43
  116.9 0.6 gather_fusion.2
  117.5 0.1 broadcast_select_fusion.2
  117.6 0.1 broadcast_select_fusion.1
  117.7 1.6 all-gather.8.cloned.1.call-done
  119.3 2.5 gather_fusion.3
  121.8 0.2 bitcast_select_fusion
  122.0 95.4 %all-gather.4.cloned.1.call-done = bf16[1024,1664]{1,0:T(8,128)(2,1)} async-done(((bf16[32,1664]{1,0:T(8,128)(2,1)}), bf16[1024,1664]{1,0:T(8,128)(2,1)}) %all-gather.4.cloned.1.call-update) | async-done | bytes 3407888 | tf_op jit(solution)/shard_map/all_gather | solution.py:61
  217.3 1.1 convert_reduce_fusion
  218.4 0.1 broadcast_compare_fusion
  218.5 0.1 broadcast_in_dim.117
  218.6 0.3 copy.18
  219.0 140.2 %all-gather.6.cloned.1.call-done = bf16[64,32,1536]{2,1,0:T(8,128)(2,1)} async-done(((bf16[4,32,1536]{2,1,0:T(8,128)(2,1)}), bf16[64,32,1536]{2,1,0:T(8,128)(2,1)}) %all-gather.6.cloned.1.call-update) | async-done | bytes 6291472 | tf_op jit(solution)/shard_map/all_gather | solution.py:41
  359.1 3.4 gather_fusion
  362.6 0.2 broadcast_select_fusion
  362.8 0.1 fusion.66
  362.9 4.0 fusion.34
  366.9 4.2 fusion.46
  371.1 0.0 copy-start.2
  371.1 4.1 fusion.31
  375.1 0.0 copy-done.2
  375.1 3.3 fusion.37
  378.5 4.1 fusion.36
  382.6 0.0 copy-done
  382.6 5.5 %add_convert_fusion = bf16[1024,1536]{1,0:T(8,128)(2,1)} fusion(f32[1024,1536]{1,0:T(8,128)} %fusion.36, bf16[1024,144]{0,1:T(8,128)(2,1)S(1)} %fusion.37, bf16[144,1536]{1,0:T(8,128)(2,1)S(1)} %copy-done), kind=kOutput, calls=%fused_computation.4 | convolution fusion | flops 456130560 | bytes 10174464 | tf_op jit(solution)/shard_map/dot_general | solution.py:96
  388.1 0.0 copy-start.1
  388.1 0.0 reduce-scatter.2.cloned.1.call-update
  388.1 133.2 %reduce-scatter.2.cloned.1.call-done = bf16[32,1536]{1,0:T(8,128)(2,1)} async-done(((bf16[1024,1536]{1,0:T(8,128)(2,1)}), bf16[32,1536]{1,0:T(8,128)(2,1)}) %reduce-scatter.2.cloned.1.call-update) | async-done | bytes 98320 | tf_op jit(solution)/shard_map/reduce_scatter | solution.py:99
  521.3 0.0 copy-done.1
  521.3 1.6 fusion.59
  (8 shorter events, 0.1 us)
Async XLA Ops:
  6.5 376.0 %copy-start = (bf16[144,1536]{1,0:T(8,128)(2,1)S(1)}, bf16[144,1536]{1,0:T(8,128)(2,1)}, u32[]{:S(2)}) copy-start(bf16[144,1536]{1,0:T(8,128)(2,1)} %param.13) | copy-start | bytes 1327108
  6.5 112.8 %all-gather.8.cloned.1.call-start = ((), (), s32[]{:S(2)}) async-start(), calls=%async_computation.3 | async-start | bytes 3342336 | tf_op jit(solution)/shard_map/all_gather | solution.py:44
  7.3 210.1 %all-gather.4.cloned.1.call-start = ((), (), s32[]{:S(2)}) async-start(), calls=%async_computation.1 | async-start | bytes 3514368 | tf_op jit(solution)/shard_map/all_gather | solution.py:61
  12.3 346.8 %all-gather.6.cloned.1.call-start = ((), (), s32[]{:S(2)}) async-start(), calls=%async_computation.2 | async-start | bytes 6684672 | tf_op jit(solution)/shard_map/all_gather | solution.py:41
  13.0 508.3 %reduce-scatter.2.cloned.1.call-start = ((), (), s32[]{:S(2)}) async-start(), calls=%async_computation.4 | async-start | bytes 3244032 | tf_op jit(solution)/shard_map/reduce_scatter | solution.py:99
  371.1 4.1 copy-start.2
  388.1 133.2 %copy-start.1 = (bf16[32,1536]{1,0:T(8,128)(2,1)S(1)}, bf16[32,1536]{1,0:T(8,128)(2,1)}, u32[]{:S(2)}) copy-start(bf16[32,1536]{1,0:T(8,128)(2,1)} %param.10) | copy-start | bytes 294916
Sparse Core Ops, SparseCore 0:
  9.4 109.8 all-gather.7
  122.7 94.6 all-gather.3
  219.4 139.6 all-gather.5
  388.2 133.0 reduce-scatter.1
where the time goes:
time: 530 us; the launch traced here: 529 us
  waiting for transfers between devices  372 us (70%)
  blocking collectives  103 us (19%)
  matrix products  25.2 us (5%)
  between operations  13.3 us (3%)
  other arithmetic  8.07 us (2%)
  local copies, waits for them, and re-layouts  7.92 us (1%)
    all_gather x1, waiting for transfers between devices, local(): lax.all_gather(adapter_gate_input, 'adp', axis=0, tiled=True)  140 us
    reduce_scatter x1, waiting for transfers between devices, local(): lax.psum_scatter(part.astype(jnp.bfloat16), 'blk', scatter_dimension=0, t...  133 us
    all_gather x1, waiting for transfers between devices, local(): gathered = lax.all_gather(packed, 'blk', axis=0, tiled=True)  95.4 us
    all_gather x1, blocking collectives, local(): lax.all_gather(adapter_gate_output, 'adp', axis=0, tiled=True)  57.1 us
    all_gather x1, blocking collectives, local(): lax.all_gather(adapter_down_input, 'adp', axis=0, tiled=True)  46 us
  transfers between devices with their start and end apart: 4, of which 4 were waited for; matrix products, arithmetic and copies ran while one was open for 2% of the time, Pallas kernels for 0%

commit v1 on v0

--- a/solution.py
+++ b/solution.py
@@ -38,7 +38,10 @@
     picked = used[None, :] & (order[None, :] == active_pos[:, None])
     active = jnp.sum(jnp.where(picked, catalog[None, :], 0), axis=1)
     every = (
-        lax.all_gather(adapter_gate_input, "adp", axis=0, tiled=True),
+        jnp.concatenate(
+            lax.all_to_all(jnp.stack([adapter_gate_input] * lax.axis_size("adp")), "adp", 0, 0),
+            axis=0,
+        ),
         lax.all_gather(adapter_gate_output, "adp", axis=0, tiled=True),
         lax.all_gather(adapter_down_input, "adp", axis=0, tiled=True),
         lax.all_gather(adapter_down_output, "adp", axis=0, tiled=True),

time: 530 us -> 482 us (0.909)
  waiting for transfers between devices: 372 us -> 171 us
  blocking collectives: 103 us -> 244 us
  starting transfers between devices: 0.12 us -> 10.4 us
    all_gather x1, blocking collectives: 57.1 us -> 211 us  [local(): lax.all_gather(adapter_gate_output, 'adp', axis=0, tiled=True)]
    all_gather x1 -> x0, waiting for transfers between devices: 140 us -> none  [local(): lax.all_gather(adapter_gate_input, 'adp', axis=0, tiled=True)]
    all_gather x1, waiting for transfers between devices: 95.4 us -> 41.8 us  [local(): gathered = lax.all_gather(packed, 'blk', axis=0, tiled=True)]
    all_gather x1, blocking collectives: 46 us -> 33.1 us  [local(): lax.all_gather(adapter_down_input, 'adp', axis=0, tiled=True)]
    all_to_all x0 -> x1, starting transfers between devices: none -> 10.3 us  [local(): lax.all_to_all(jnp.stack([adapter_gate_input] * lax.axis_size('adp')), 'a...]
  transfers between devices with their start and end apart: 4 -> 4, of which waited for: 4 -> 2; matrix products, arithmetic and copies ran while one was open for 2% -> 2% of each run, Pallas kernels for 0% -> 0%
where the time goes in v1:
time: 482 us; the launch traced here: 481 us
  blocking collectives  244 us (51%)
  waiting for transfers between devices  171 us (35%)
  matrix products  24.2 us (5%)
  between operations  13.4 us (3%)
  local copies, waits for them, and re-layouts  12.5 us (3%)
  starting transfers between devices  10.4 us (2%)
  other arithmetic  5.53 us (1%)
    all_gather x1, blocking collectives, local(): lax.all_gather(adapter_gate_output, 'adp', axis=0, tiled=True)  211 us
    reduce_scatter x1, waiting for transfers between devices, local(): lax.psum_scatter(part.astype(jnp.bfloat16), 'blk', scatter_dimension=0, t...  129 us
    all_gather x1, waiting for transfers between devices, local(): gathered = lax.all_gather(packed, 'blk', axis=0, tiled=True)  41.8 us
    all_gather x1, blocking collectives, local(): lax.all_gather(adapter_down_input, 'adp', axis=0, tiled=True)  33.1 us
    all_to_all x1, starting transfers between devices, local(): lax.all_to_all(jnp.stack([adapter_gate_input] * lax.axis_size('adp')), 'a...  10.3 us
  transfers between devices with their start and end apart: 4, of which 2 were waited for; matrix products, arithmetic and copies ran while one was open for 2% of the time, Pallas kernels for 0%

profile of v1, /device:TPU:8, one launch (start us, length us, event | category | flops | bytes accessed | tf_op | source)
XLA Modules:
  0.0 481.4 jit_solution(11043996429032792005)
XLA Ops:
  6.5 0.0 copy-start
  6.5 0.0 all-gather.5.cloned.1.call-start
  6.5 0.7 all-gather.5.cloned.1.call-update
  7.3 4.4 stack.2
  11.7 0.0 copy-start.7
  11.7 0.0 copy-start.8
  11.7 0.0 copy-start.1
  11.7 0.0 copy-start.2
  11.7 0.0 copy-start.3
  11.7 10.3 %all-to-all-start = ((bf16[16,4,32,1536]{3,2,1,0:T(8,128)(2,1)}), bf16[16,4,32,1536]{3,2,1,0:T(8,128)(2,1)}, u32[]{:S(2)}, u32[]{:S(2)}) async-start(bf16[16,4,32,1536]{3,2,1,0:T(8,128)(2,1)} %stack.2), calls=%async_computation | async-start | bytes 12582912 | tf_op jit(solution)/shard_map/all_to_all | solution.py:42
  22.0 0.0 all-gather.3.cloned.1.call-start
  22.1 0.0 copy-done.7
  22.1 0.1 fusion.60
  22.2 0.1 copy.17
  22.3 0.1 reduce-window.8
  22.4 0.1 add_reduce_fusion
  22.5 0.1 select_reduce_fusion.2
  22.6 0.0 copy-done.8
  22.7 0.2 select_reduce_fusion
  22.8 0.1 select_reduce_fusion.1
  22.9 0.0 copy-done.1
  23.0 0.1 fusion.56
  23.1 0.0 copy-done.5
  23.1 0.1 fusion.58
  23.2 0.1 broadcast_in_dim.116
  23.3 0.6 pad_maximum_fusion
  23.9 0.0 all-gather.3.cloned.1.call-update
  23.9 0.0 reduce-scatter.2.cloned.1.call-start
  24.0 0.0 copy-start.6
  24.0 0.1 broadcast_in_dim.125
  24.1 0.1 broadcast_in_dim.126
  24.2 0.0 copy-done.2
  24.2 0.0 copy-start.4
  24.2 211.0 %all_gather.13 = bf16[64,2,16,144]{3,2,1,0:T(8,128)(2,1)S(1)} all-gather(bf16[4,2,16,144]{3,2,1,0:T(8,128)(2,1)S(1)} %copy-done.2), channel_id=1, replica_groups=mesh['blk'=32,'adp'=16] {'adp'}, dimensions={0}, use_global_device_ids=true | all-gather | bytes 626688 | tf_op jit(solution)/shard_map/all_gather | solution.py:45
  235.2 0.6 gather_fusion.1
  235.8 0.0 copy-done.3
  235.8 33.1 %all_gather.14 = bf16[64,144,16]{1,2,0:T(8,128)(2,1)S(1)} all-gather(bf16[4,144,16]{1,2,0:T(8,128)(2,1)S(1)} %copy-done.3), channel_id=1, replica_groups=mesh['blk'=32,'adp'=16] {'adp'}, dimensions={0}, use_global_device_ids=true | all-gather | bytes 313344 | tf_op jit(solution)/shard_map/all_gather | solution.py:46
  268.9 0.6 gather_fusion.2
  269.4 0.1 broadcast_select_fusion.2
  269.5 0.1 broadcast_select_fusion.1
  269.6 0.0 copy-done.6
  269.7 0.0 all-gather.5.cloned.1.call-done
  269.7 2.5 gather_fusion.3
  272.2 0.2 bitcast_select_fusion
  272.3 0.0 copy-done.4
  272.4 41.8 %all-gather.3.cloned.1.call-done = bf16[1024,1664]{1,0:T(8,128)(2,1)} async-done(((bf16[32,1664]{1,0:T(8,128)(2,1)}), bf16[1024,1664]{1,0:T(8,128)(2,1)}) %all-gather.3.cloned.1.call-update) | async-done | bytes 3407888 | tf_op jit(solution)/shard_map/all_gather | solution.py:64
  314.2 1.1 convert_reduce_fusion
  315.3 0.1 broadcast_compare_fusion
  315.3 0.1 broadcast_in_dim.117
  315.4 0.3 copy.18
  315.8 0.0 all-to-all-done
  315.8 3.6 gather_fusion
  319.4 0.8 broadcast_select_fusion
  320.2 0.1 fusion.66
  320.3 4.0 fusion.34
  324.3 3.4 fusion.46
  327.7 4.0 fusion.31
  331.7 3.3 fusion.37
  335.0 4.1 fusion.36
  339.1 0.0 copy-done
  339.1 5.5 %add_convert_fusion = bf16[1024,1536]{1,0:T(8,128)(2,1)} fusion(f32[1024,1536]{1,0:T(8,128)} %fusion.36, bf16[1024,144]{0,1:T(8,128)(2,1)S(1)} %fusion.37, bf16[144,1536]{1,0:T(8,128)(2,1)S(1)} %copy-done), kind=kOutput, calls=%fused_computation.4 | convolution fusion | flops 456130560 | bytes 10174464 | tf_op jit(solution)/shard_map/dot_general | solution.py:99
  344.6 0.0 reduce-scatter.2.cloned.1.call-update
  344.6 128.6 %reduce-scatter.2.cloned.1.call-done = bf16[32,1536]{1,0:T(8,128)(2,1)} async-done(((bf16[1024,1536]{1,0:T(8,128)(2,1)}), bf16[32,1536]{1,0:T(8,128)(2,1)}) %reduce-scatter.2.cloned.1.call-update) | async-done | bytes 98320 | tf_op jit(solution)/shard_map/reduce_scatter | solution.py:102
  473.3 1.6 fusion.59
  (9 shorter events, 0.1 us)
Async XLA Ops:
  6.5 332.5 %copy-start = (bf16[144,1536]{1,0:T(8,128)(2,1)S(1)}, bf16[144,1536]{1,0:T(8,128)(2,1)}, u32[]{:S(2)}) copy-start(bf16[144,1536]{1,0:T(8,128)(2,1)} %param.13) | copy-start | bytes 1327108
  6.5 263.1 %all-gather.5.cloned.1.call-start = ((), (), s32[]{:S(2)}) async-start(), calls=%async_computation.3 | async-start | bytes 3342336 | tf_op jit(solution)/shard_map/all_gather | solution.py:47
  11.7 10.4 %copy-start.7 = (s32[256]{0:T(256)S(1)}, s32[256]{0:T(256)}, u32[]{:S(2)}) copy-start(s32[256]{0:T(256)} %param.18) | copy-start | bytes 3076
  11.7 11.0 %copy-start.8 = (s32[32]{0:T(128)S(1)}, s32[32]{0:T(128)}, u32[]{:S(2)}) copy-start(s32[32]{0:T(128)} %param.19) | copy-start | bytes 388
  11.7 11.3 %copy-start.1 = (bf16[32,1536]{1,0:T(8,128)(2,1)S(1)}, bf16[32,1536]{1,0:T(8,128)(2,1)}, u32[]{:S(2)}) copy-start(bf16[32,1536]{1,0:T(8,128)(2,1)} %param.10) | copy-start | bytes 294916
  11.7 11.4 %copy-start.5 = (f32[1536]{0:T(1024)S(1)}, f32[1536]{0:T(1024)}, u32[]{:S(2)}) copy-start(f32[1536]{0:T(1024)} %param.11) | copy-start | bytes 18436
  11.7 12.5 %copy-start.2 = (bf16[4,2,16,144]{3,2,1,0:T(8,128)(2,1)S(1)}, bf16[4,2,16,144]{3,2,1,0:T(8,128)(2,1)}, u32[]{:S(2)}) copy-start(bf16[4,2,16,144]{3,2,1,0:T(8,128)(2,1)} %param.15) | copy-start | bytes 110596
  11.7 224.1 %copy-start.3 = (bf16[4,144,16]{1,2,0:T(8,128)(2,1)S(1)}, bf16[4,144,16]{1,2,0:T(8,128)(2,1)}, u32[]{:S(2)}) copy-start(bf16[4,144,16]{1,2,0:T(8,128)(2,1)} %param.16) | copy-start | bytes 55300
  11.7 304.1 %all-to-all-start = ((bf16[16,4,32,1536]{3,2,1,0:T(8,128)(2,1)}), bf16[16,4,32,1536]{3,2,1,0:T(8,128)(2,1)}, u32[]{:S(2)}, u32[]{:S(2)}) async-start(bf16[16,4,32,1536]{3,2,1,0:T(8,128)(2,1)} %stack.2), calls=%async_computation | async-start | bytes 12582912 | tf_op jit(solution)/shard_map/all_to_all | solution.py:42
  22.0 292.1 %all-gather.3.cloned.1.call-start = ((), (), s32[]{:S(2)}) async-start(), calls=%async_computation.2 | async-start | bytes 3514368 | tf_op jit(solution)/shard_map/all_gather | solution.py:64
  23.9 449.3 %reduce-scatter.2.cloned.1.call-start = ((), (), s32[]{:S(2)}) async-start(), calls=%async_computation.4 | async-start | bytes 3244032 | tf_op jit(solution)/shard_map/reduce_scatter | solution.py:102
  24.0 245.6 %copy-start.6 = (pred[16]{0:T(512)(128)(4,1)}, pred[16]{0:T(512)(128)(4,1)S(1)}, u32[]{:S(2)}) copy-start(pred[16]{0:T(512)(128)(4,1)S(1)} %compare_and_fusion) | copy-start | bytes 52
  24.2 248.1 %copy-start.4 = (s32[1024]{0:T(1024)}, s32[1024]{0:T(1024)S(1)}, u32[]{:S(2)}) copy-start(s32[1024]{0:T(1024)S(1)} %pad_clamp_fusion) | copy-start | bytes 12292
Sparse Core Ops, SparseCore 0:
  9.4 194.9 all-gather.4
  207.8 106.3 all-gather.2
  344.7 128.4 reduce-scatter.1
